TPU v7x, 32 devices: a whole 2x2x4 slice. The times are simulated.
32 devices in a mesh: seg: 8 (over y, x, core), head: 4 (over z).
Axes of the slice: x: 2, y: 2, z: 4, core: 2. Of those that a mesh axis runs over, the one named last changes fastest.
Arguments:
- layer_input: bfloat16 [1, 4096, 2048], P(None, 'seg', 'head'), may hold values from -160 to 160, as said below
- w_qkv: bfloat16 [2048, 3, 1024], P(None, None, 'head'), may hold values from -3 to 3
- comp_weight: bfloat16 [3, 2, 1024], P(None, None, 'head'), may hold values from -2.5 to 2.5
- w_out: bfloat16 [1024, 2048], P('seg', 'head'), may hold values from -1.5 to 1.5
Outputs:
- attn_out: bfloat16 [1, 4096, 2048], P(None, 'seg', 'head')
Inputs may be any that keep to these rules, and one draw needn't show every extreme that they name: layer_input varies in scale from feature to feature and from token to token.
All inputs are finite; a program needn't handle non-finite values.
Results may differ from a plain program's by a relative error of at most 0.0089.
Values may be sent and summed in bfloat16 or wider, within the bound.
No kernel may reach another device: no remote copies, remote signals or barrier semaphores. Data moves between devices by JAX's collectives and lax.ppermute only.
A program may use at most 64 MiB of HBM per device.

v0:
```python
import math
import jax
import jax.numpy as jnp
from jax import lax
from jax.sharding import PartitionSpec as P

DH = 128


def passed_along(block, axis, distance):
    devices = range(lax.axis_size(axis))
    route = [(i - distance, i) for i in devices if i - distance in devices]
    return lax.ppermute(block, axis, route)


def layer_norm(values):
    center_mean = jnp.mean(values, axis=-1, keepdims=True)
    centered = values - center_mean
    variance = jnp.mean(centered * centered, axis=-1, keepdims=True)
    return centered * lax.rsqrt(variance + 1e-05)


def compress_block(source, weight):
    batch, pair, length, width = source.shape
    grouped = source.reshape(batch, pair, length // 3, 3, width)
    mixed = jnp.einsum("bkltc,tkc->bklc", grouped, weight, preferred_element_type=jnp.float32)
    return mixed.astype(jnp.bfloat16)


def key_allowed(seg_len, segment):
    query_pos = jnp.arange(seg_len)[:, None]
    key_pos = jnp.arange(3 * seg_len)[None, :]
    own_part = (key_pos >= 2 * seg_len) & (key_pos - 2 * seg_len <= query_pos)
    memory_part = (key_pos >= seg_len) & (key_pos < 2 * seg_len) & (segment >= 1)
    comp_part = (key_pos < seg_len) & (segment >= 4)
    return own_part | memory_part | comp_part


def attend(queries, key_vals, segment):
    batch, seg_len, width = queries.shape
    heads_here = width // DH
    query_heads = queries.reshape(batch, seg_len, heads_here, DH)
    key_heads = key_vals[:, 0].reshape(batch, 3 * seg_len, heads_here, DH)
    value_heads = key_vals[:, 1].reshape(batch, 3 * seg_len, heads_here, DH)
    scores = jnp.einsum(
        "bqhd,bkhd->bhqk", query_heads, key_heads, preferred_element_type=jnp.float32
    )
    scores = scores / math.sqrt(DH)
    allowed = key_allowed(seg_len, segment)
    scores = jnp.where(allowed[None, None], scores, jnp.float32(-1e30))
    highest = jnp.max(scores, axis=-1, keepdims=True)
    exponent = jnp.exp(scores - highest)
    weights = (exponent / jnp.sum(exponent, axis=-1, keepdims=True)).astype(jnp.bfloat16)
    mixed = jnp.einsum("bhqk,bkhd->bqhd", weights, value_heads, preferred_element_type=jnp.float32)
    return mixed.astype(jnp.bfloat16).reshape(batch, seg_len, width)


def local(layer_input, w_qkv, comp_weight, w_out):
    gathered = lax.all_gather(layer_input, "head", axis=2, tiled=True)
    normed = layer_norm(gathered.astype(jnp.float32)).astype(jnp.bfloat16)
    projected = jnp.einsum("bld,dkc->bklc", normed, w_qkv, preferred_element_type=jnp.float32)
    projected = projected.astype(jnp.bfloat16)
    queries = projected[:, 0]
    key_vals = projected[:, 1:3]
    memory = passed_along(key_vals, "seg", 1)
    second_back = passed_along(memory, "seg", 1)
    upcoming = compress_block(jnp.concatenate([second_back, memory, key_vals], axis=2), comp_weight)
    compressed = passed_along(upcoming, "seg", 2)
    segment = lax.axis_index("seg")
    joined = jnp.concatenate([compressed, memory, key_vals], axis=2)
    context = attend(queries, joined, segment)
    full_ctx = lax.all_gather(context, "head", axis=2, tiled=True)
    whole_out = lax.all_gather(w_out, "seg", axis=0, tiled=True)
    result_sum = jnp.einsum("blr,rc->blc", full_ctx, whole_out, preferred_element_type=jnp.float32)
    return result_sum.astype(jnp.bfloat16)


def solution(mesh):
    return jax.shard_map(
        local,
        mesh=mesh,
        in_specs=(
            P(None, "seg", "head"),
            P(None, None, "head"),
            P(None, None, "head"),
            P("seg", "head"),
        ),
        out_specs=P(None, "seg", "head"),
        check_vma=False,
    )
```

profile of v0, /device:TPU:0, one launch (start us, length us, event | category | flops | bytes accessed | tf_op | source)
XLA Modules:
  0.0 164.3 jit_solution(6512609901003673193)
XLA Ops:
  7.4 0.0 copy-start
  7.4 0.0 all-gather.4.cloned.1.call-start
  7.4 0.7 all-gather.4.cloned.1.call-update
  8.1 0.0 all-gather.8.cloned.1.call-start
  8.1 50.0 %all-gather.4.cloned.1.call-done = bf16[1,512,2048]{2,1,0:T(8,128)(2,1)} async-done(((bf16[1,512,512]{2,1,0:T(8,128)(2,1)}), bf16[1,512,2048]{2,1,0:T(8,128)(2,1)}) %all-gather.4.cloned.1.call-update) | async-done | bytes 2097168 | tf_op jit(solution)/shard_map/all_gather | solution.py:59
  58.1 0.0 copy-start.1
  58.2 2.1 %convert_reduce_fusion = f32[512]{0:T(512)S(1)} fusion(bf16[1,512,2048]{2,1,0:T(8,128)(2,1)} %all-gather.4.cloned.1.call-done), kind=kLoop, calls=%fused_computation.6 | loop fusion | flops 2096640 | bytes 2099200 | tf_op jit(solution)/shard_map/reduce_sum | solution.py:17
  60.3 0.1 copy-done.1
  60.4 0.7 fusion.4
  61.1 0.0 copy-done
  61.1 0.0 copy-start.4
  61.1 2.0 %fusion.21 = bf16[1,3,512,256]{2,3,1,0:T(8,128)(2,1)S(1)} fusion(bf16[2048,3,256]{2,0,1:T(8,128)(2,1)S(1)} %copy-done, bf16[1,512,2048]{2,1,0:T(8,128)(2,1)S(1)} %copy-done.1, f32[512]{0:T(512)S(1)} %add_rsqrt_fusion, f32[512]{0:T(512)S(1)} %broadcast_multiply_fusion), kind=kOutput, calls=%fused_computation.29 | convolution fusion | flops 1615200256 | bytes 6033408 | tf_op jit(solution)/shard_map/bld,dkc->bklc/dot_general | solution.py:61
  63.1 0.0 copy-start.3
  63.1 0.0 copy-start.2
  63.1 0.8 copy-done.2
  64.0 2.4 %collective-permute-start = (bf16[1,2,512,256]{2,3,1,0:T(8,128)(2,1)S(1)}, bf16[1,2,512,256]{2,3,1,0:T(8,128)(2,1)}, u32[]{:S(2)}, u32[]{:S(2)}) collective-permute-start(bf16[1,2,512,256]{2,3,1,0:T(8,128)(2,1)S(1)} %slice.16), channel_id=1, source_target_pairs={{0,4},{4,8},{8,12},{12,16},{16,20},{20,24},{24,28},{1,5},{5,9},{9,... | collective-permute-start | bytes 1572872 | tf_op jit(solution)/shard_map/ppermute | solution.py:13
  66.4 0.8 collective-permute-done
  67.2 0.0 copy-done.3
  67.2 9.1 %collective-permute-start.1 = (bf16[1,2,512,256]{2,3,1,0:T(8,128)(2,1)}, bf16[1,2,512,256]{2,3,1,0:T(8,128)(2,1)}, u32[]{:S(2)}, u32[]{:S(2)}) collective-permute-start(bf16[1,2,512,256]{2,3,1,0:T(8,128)(2,1)} %collective-permute-done), channel_id=1, source_target_pairs={{0,4},{4,8},{8,12},{12,16},{16,20},{20,24},{24,28},{1,5},{5,9},{9,... | collective-permute-start | bytes 1572872 | tf_op jit(solution)/shard_map/ppermute | solution.py:13
  76.3 0.0 all-gather.8.cloned.1.call-update
  76.3 0.0 all-gather.6.cloned.1.call-start
  76.4 0.0 copy-done.4
  76.4 0.9 collective-permute-done.1
  77.3 2.6 %pad_maximum_fusion.1 = bf16[1,2,1536,256]{2,3,1,0:T(8,128)(2,1)} fusion(bf16[1,2,512,256]{2,3,1,0:T(8,128)(2,1)} %copy-done.2, bf16[1,2,512,256]{2,3,1,0:T(8,128)(2,1)} %collective-permute-done, bf16[1,2,512,256]{2,3,1,0:T(8,128)(2,1)} %collective-permute-done.1), kind=kLoop, calls=%fused_computation.25 | loop fusion | flops 4718592 | bytes 3145728 | tf_op jit(solution)/shard_map/concatenate | solution.py:67
  80.0 4.9 %copy.23 = bf16[1,2,1536,256]{3,1,2,0:T(2,128)(2,1)} copy(bf16[1,2,1536,256]{2,3,1,0:T(8,128)(2,1)} %pad_maximum_fusion.1) | data formatting | bytes 3145728
  84.9 5.0 %multiply_reduce_fusion = bf16[2,256,512]{1,0,2:T(2,128)(2,1)} fusion(bf16[2,256,3,512]{1,0,2,3:T(2,128)(2,1)} %bitcast.45, f32[2,256,3]{1,0,2:T(2,128)S(1)} %bitcast_convert_fusion), kind=kLoop, calls=%fused_computation.11 | loop fusion | flops 2097152 | bytes 2103296
  89.9 2.0 %copy.20 = bf16[2,256,512]{2,1,0:T(8,128)(2,1)} copy(bf16[2,256,512]{1,0,2:T(2,128)(2,1)} %multiply_reduce_fusion) | data formatting | bytes 1048576 | tf_op jit(solution)/shard_map/bkltc,tkc->bklc/dot_general | solution.py:26
  91.9 11.8 %collective-permute-start.2 = (bf16[1,2,512,256]{2,3,1,0:T(8,128)(2,1)}, bf16[1,2,512,256]{2,3,1,0:T(8,128)(2,1)S(1)}, u32[]{:S(2)}, u32[]{:S(2)}) collective-permute-start(bf16[1,2,512,256]{2,3,1,0:T(8,128)(2,1)} %bitcast.49), channel_id=1, source_target_pairs={{0,8},{4,12},{8,16},{12,20},{16,24},{20,28},{1,9},{5,13},{9,17},{1... | collective-permute-start | bytes 1572872 | tf_op jit(solution)/shard_map/ppermute | solution.py:13
  103.7 1.6 fusion.10
  105.3 1.0 slice.18
  106.3 9.7 %collective-permute-done.2 = bf16[1,2,512,256]{2,3,1,0:T(8,128)(2,1)S(1)} collective-permute-done((bf16[1,2,512,256]{2,3,1,0:T(8,128)(2,1)}, bf16[1,2,512,256]{2,3,1,0:T(8,128)(2,1)S(1)}, u32[]{:S(2)}, u32[]{:S(2)}) %collective-permute-start.2) | collective-permute-done | bytes 524320 | tf_op jit(solution)/shard_map/ppermute | solution.py:13
  116.0 1.3 pad_maximum_fusion
  117.3 1.3 fusion.39
  118.6 3.8 %fusion.40 = f32[2,512]{1,0:T(2,128)S(1)} fusion(pred[512,1536]{1,0:T(8,128)(4,1)} %fusion.10, bf16[512,2,128]{0,2,1:T(8,128)(2,1)S(1)} %bitcast.50, bf16[1536,2,128]{0,2,1:T(8,128)(2,1)} %bitcast.46), kind=kOutput, calls=%fused_computation.53 | convolution fusion | flops 408946176 | bytes 1839104 | tf_op jit(solution)/shard_map/sub | solution.py:52
  122.5 5.2 %fusion.25 = bf16[2,128,512]{2,1,0:T(8,128)(2,1)} fusion(bf16[1536,2,128]{0,2,1:T(8,128)(2,1)} %bitcast.48, f32[2,512]{1,0:T(2,128)S(1)} %fusion.40, pred[512,1536]{1,0:T(8,128)(4,1)} %fusion.10, bf16[512,2,128]{0,2,1:T(8,128)(2,1)S(1)} %bitcast.51, bf16[1536,2,128]{0,2,1:T(8,128)(2,1)} %bitcast.47), kind=kOutput, calls=%fused_computation.32 | convolution fusion | flops 813304320 | bytes 2887680 | tf_op jit(solution)/shard_map/bhqk,bkhd->bqhd/dot_general | solution.py:54
  127.6 0.0 all-gather.6.cloned.1.call-update
  127.7 0.0 all-gather.8.cloned.1.call-done
  127.7 26.1 %all-gather.6.cloned.1.call-done = bf16[1,512,1024]{1,2,0:T(8,128)(2,1)} async-done(((bf16[1,512,256]{1,2,0:T(8,128)(2,1)}), bf16[1,512,1024]{1,2,0:T(8,128)(2,1)}) %all-gather.6.cloned.1.call-update) | async-done | bytes 1048592 | tf_op jit(solution)/shard_map/all_gather | solution.py:72
  153.8 3.1 %fusion.24 = bf16[1,512,512]{2,1,0:T(8,128)(2,1)} fusion(bf16[1024,512]{1,0:T(8,128)(2,1)} %all-gather.8.cloned.1.call-done, bf16[1,512,1024]{1,2,0:T(8,128)(2,1)} %all-gather.6.cloned.1.call-done), kind=kOutput, calls=%fused_computation.31 | convolution fusion | flops 537133056 | bytes 2621440 | tf_op jit(solution)/shard_map/blr,rc->blc/dot_general | solution.py:74
  (7 shorter events, 0.1 us)
Async XLA Ops:
  7.4 53.7 %copy-start = (bf16[2048,3,256]{2,0,1:T(8,128)(2,1)S(1)}, bf16[2048,3,256]{2,0,1:T(8,128)(2,1)}, u32[]{:S(2)}) copy-start(bf16[2048,3,256]{2,0,1:T(8,128)(2,1)} %param.5) | copy-start | bytes 9437188
  7.4 50.8 %all-gather.4.cloned.1.call-start = ((), (), s32[]{:S(2)}) async-start(), calls=%async_computation | async-start | bytes 2621440 | tf_op jit(solution)/shard_map/all_gather | solution.py:59
  8.1 119.6 %all-gather.8.cloned.1.call-start = ((), (), s32[]{:S(2)}) async-start(), calls=%async_computation.2 | async-start | bytes 1179648 | tf_op jit(solution)/shard_map/all_gather | solution.py:73
  58.1 2.2 %copy-start.1 = (bf16[1,512,2048]{2,1,0:T(8,128)(2,1)S(1)}, bf16[1,512,2048]{2,1,0:T(8,128)(2,1)}, u32[]{:S(2)}) copy-start(bf16[1,512,2048]{2,1,0:T(8,128)(2,1)} %all-gather.4.cloned.1.call-done) | copy-start | bytes 6291460
  61.1 15.3 %copy-start.4 = (bf16[3,2,256]{2,1,0:T(2,128)(2,1)S(1)}, bf16[3,2,256]{2,1,0:T(2,128)(2,1)}, u32[]{:S(2)}) copy-start(bf16[3,2,256]{2,1,0:T(2,128)(2,1)} %param.6) | copy-start | bytes 9220
  63.1 4.1 %copy-start.3 = (bf16[1,3,512,256]{2,3,1,0:T(8,128)(2,1)}, bf16[1,3,512,256]{2,3,1,0:T(8,128)(2,1)S(1)}, u32[]{:S(2)}) copy-start(bf16[1,3,512,256]{2,3,1,0:T(8,128)(2,1)S(1)} %fusion.21) | copy-start | bytes 2359300
  63.1 0.9 copy-start.2
  64.0 3.2 %collective-permute-start = (bf16[1,2,512,256]{2,3,1,0:T(8,128)(2,1)S(1)}, bf16[1,2,512,256]{2,3,1,0:T(8,128)(2,1)}, u32[]{:S(2)}, u32[]{:S(2)}) collective-permute-start(bf16[1,2,512,256]{2,3,1,0:T(8,128)(2,1)S(1)} %slice.16), channel_id=1, source_target_pairs={{0,4},{4,8},{8,12},{12,16},{16,20},{20,24},{24,28},{1,5},{5,9},{9,... | collective-permute-start | bytes 1572872 | tf_op jit(solution)/shard_map/ppermute | solution.py:13
  67.2 10.1 %collective-permute-start.1 = (bf16[1,2,512,256]{2,3,1,0:T(8,128)(2,1)}, bf16[1,2,512,256]{2,3,1,0:T(8,128)(2,1)}, u32[]{:S(2)}, u32[]{:S(2)}) collective-permute-start(bf16[1,2,512,256]{2,3,1,0:T(8,128)(2,1)} %collective-permute-done), channel_id=1, source_target_pairs={{0,4},{4,8},{8,12},{12,16},{16,20},{20,24},{24,28},{1,5},{5,9},{9,... | collective-permute-start | bytes 1572872 | tf_op jit(solution)/shard_map/ppermute | solution.py:13
  76.3 77.5 %all-gather.6.cloned.1.call-start = ((), (), s32[]{:S(2)}) async-start(), calls=%async_computation.1 | async-start | bytes 1310720 | tf_op jit(solution)/shard_map/all_gather | solution.py:72
  91.9 24.1 %collective-permute-start.2 = (bf16[1,2,512,256]{2,3,1,0:T(8,128)(2,1)}, bf16[1,2,512,256]{2,3,1,0:T(8,128)(2,1)S(1)}, u32[]{:S(2)}, u32[]{:S(2)}) collective-permute-start(bf16[1,2,512,256]{2,3,1,0:T(8,128)(2,1)} %bitcast.49), channel_id=1, source_target_pairs={{0,8},{4,12},{8,16},{12,20},{16,24},{20,28},{1,9},{5,13},{9,17},{1... | collective-permute-start | bytes 1572872 | tf_op jit(solution)/shard_map/ppermute | solution.py:13
Sparse Core Ops, SparseCore 0:
  9.7 48.3 all-gather.3
Sparse Core Ops, SparseCore 1:
  76.4 23.4 all-gather.7
  127.7 26.0 all-gather.5
where the time goes:
time: 165 us; the launch traced here: 164 us
  waiting for transfers between devices  88.4 us (54%)
  starting transfers between devices  23.3 us (14%)
  between operations  15 us (9%)
  matrix products  14.1 us (9%)
  other arithmetic  13.4 us (8%)
  local copies, waits for them, and re-layouts  10.2 us (6%)
    all_gather x1, waiting for transfers between devices, local(): gathered = lax.all_gather(layer_input, 'head', axis=2, tiled=True)  50 us
    all_gather x1, waiting for transfers between devices, local(): full_ctx = lax.all_gather(context, 'head', axis=2, tiled=True)  26.1 us
    ppermute x3, starting transfers between devices, passed_along(): return lax.ppermute(block, axis, route)  23.2 us
    ppermute x3, waiting for transfers between devices, passed_along(): return lax.ppermute(block, axis, route)  11.5 us
    unnamed x11, local copies, waits for them, and re-layouts  5.9 us
    dot_general x1, matrix products, attend(): jnp.einsum('bhqk,bkhd->bqhd', weights, value_heads, preferred_element_typ...  5.18 us
    unnamed x2, other arithmetic  5.02 us
    sub x1, matrix products, attend(): exponent = jnp.exp(scores - highest)  3.83 us
  transfers between devices with their start and end apart: 6, of which 5 were waited for; matrix products, arithmetic and copies ran while one was open for 18% of the time, Pallas kernels for 0%

commit v1 on v0

--- a/solution.py
+++ b/solution.py
@@ -69,7 +69,17 @@
     segment = lax.axis_index("seg")
     joined = jnp.concatenate([compressed, memory, key_vals], axis=2)
     context = attend(queries, joined, segment)
-    full_ctx = lax.all_gather(context, "head", axis=2, tiled=True)
+    world_n = lax.axis_size("head")
+    aux = sorted(((ii, (ii + 1) % world_n) for ii in range(world_n)))
+    u_next = context
+    pages = [u_next]
+    dev = 1
+    while dev < world_n:
+        u_next = lax.ppermute(u_next, "head", aux)
+        pages.insert(0, u_next)
+        dev = dev + 1
+    high = jnp.concatenate(pages, 2)
+    full_ctx = jnp.roll(high, (lax.axis_index("head") + 1) * context.shape[2], 2)
     whole_out = lax.all_gather(w_out, "seg", axis=0, tiled=True)
     result_sum = jnp.einsum("blr,rc->blc", full_ctx, whole_out, preferred_element_type=jnp.float32)
     return result_sum.astype(jnp.bfloat16)

time: 165 us -> 177 us (1.073)
  local copies, waits for them, and re-layouts: 10.2 us -> 21.4 us
  waiting for transfers between devices: 88.4 us -> 90.3 us
    ppermute x0 -> x3, waiting for transfers between devices: none -> 28 us  [local(): u_next = lax.ppermute(u_next, 'head', aux)]
    all_gather x1 -> x0, waiting for transfers between devices: 26.1 us -> none  [local(): full_ctx = lax.all_gather(context, 'head', axis=2, tiled=True)]
    unnamed x11 -> x24, local copies, waits for them, and re-layouts: 5.9 us -> 16.4 us
  transfers between devices with their start and end apart: 6 -> 8, of which waited for: 5 -> 7; matrix products, arithmetic and copies ran while one was open for 18% -> 22% of each run, Pallas kernels for 0% -> 0%
where the time goes in v1:
time: 177 us
  waiting for transfers between devices  90.3 us (51%)
  starting transfers between devices  23.3 us (13%)
  local copies, waits for them, and re-layouts  21.4 us (12%)
  between operations  15 us (8%)
  other arithmetic  13.4 us (8%)
  matrix products  13.4 us (8%)
    all_gather x1, waiting for transfers between devices, local(): gathered = lax.all_gather(layer_input, 'head', axis=2, tiled=True)  50 us
    ppermute x3, waiting for transfers between devices, local(): u_next = lax.ppermute(u_next, 'head', aux)  28 us
    ppermute x3, starting transfers between devices, passed_along(): return lax.ppermute(block, axis, route)  23.2 us
    unnamed x24, local copies, waits for them, and re-layouts  16.4 us
    ppermute x3, waiting for transfers between devices, passed_along(): return lax.ppermute(block, axis, route)  11.5 us
    unnamed x2, other arithmetic  5.04 us
    dot_general x1, matrix products, attend(): jnp.einsum('bhqk,bkhd->bqhd', weights, value_heads, preferred_element_typ...  4.55 us
    sub x1, matrix products, attend(): exponent = jnp.exp(scores - highest)  3.83 us
  transfers between devices with their start and end apart: 8, of which 7 were waited for; matrix products, arithmetic and copies ran while one was open for 22% of the time, Pallas kernels for 0%

profile of v1, /device:TPU:0, one launch (start us, length us, event | category | flops | bytes accessed | tf_op | source)
XLA Modules:
  0.0 176.8 jit_solution(14255322545353823871)
XLA Ops:
  7.4 0.0 copy-start
  7.4 0.0 all-gather.3.cloned.1.call-start
  7.4 0.7 all-gather.3.cloned.1.call-update
  8.1 0.0 all-gather.5.cloned.1.call-start
  8.1 50.0 %all-gather.3.cloned.1.call-done = bf16[1,512,2048]{2,1,0:T(8,128)(2,1)} async-done(((bf16[1,512,512]{2,1,0:T(8,128)(2,1)}), bf16[1,512,2048]{2,1,0:T(8,128)(2,1)}) %all-gather.3.cloned.1.call-update) | async-done | bytes 2097168 | tf_op jit(solution)/shard_map/all_gather | solution.py:59
  58.1 0.0 copy-start.1
  58.2 2.1 %convert_reduce_fusion = f32[512]{0:T(512)S(1)} fusion(bf16[1,512,2048]{2,1,0:T(8,128)(2,1)} %all-gather.3.cloned.1.call-done), kind=kLoop, calls=%fused_computation.6 | loop fusion | flops 2096640 | bytes 2099200 | tf_op jit(solution)/shard_map/reduce_sum | solution.py:17
  60.3 0.1 copy-done.1
  60.4 0.7 fusion.4
  61.1 0.0 copy-done
  61.1 0.0 copy-start.7
  61.1 2.0 %fusion.21 = bf16[1,3,512,256]{2,3,1,0:T(8,128)(2,1)S(1)} fusion(bf16[2048,3,256]{2,0,1:T(8,128)(2,1)S(1)} %copy-done, bf16[1,512,2048]{2,1,0:T(8,128)(2,1)S(1)} %copy-done.1, f32[512]{0:T(512)S(1)} %add_rsqrt_fusion, f32[512]{0:T(512)S(1)} %broadcast_multiply_fusion), kind=kOutput, calls=%fused_computation.29 | convolution fusion | flops 1615200256 | bytes 6033408 | tf_op jit(solution)/shard_map/bld,dkc->bklc/dot_general | solution.py:61
  63.1 0.0 copy-start.5
  63.1 0.0 copy-start.2
  63.1 0.8 copy-done.2
  64.0 2.4 %collective-permute-start = (bf16[1,2,512,256]{2,3,1,0:T(8,128)(2,1)S(1)}, bf16[1,2,512,256]{2,3,1,0:T(8,128)(2,1)}, u32[]{:S(2)}, u32[]{:S(2)}) collective-permute-start(bf16[1,2,512,256]{2,3,1,0:T(8,128)(2,1)S(1)} %slice.16), channel_id=1, source_target_pairs={{0,4},{4,8},{8,12},{12,16},{16,20},{20,24},{24,28},{1,5},{5,9},{9,... | collective-permute-start | bytes 1572872 | tf_op jit(solution)/shard_map/ppermute | solution.py:13
  66.4 0.9 collective-permute-done
  67.2 0.0 copy-done.5
  67.2 9.1 %collective-permute-start.1 = (bf16[1,2,512,256]{2,3,1,0:T(8,128)(2,1)}, bf16[1,2,512,256]{2,3,1,0:T(8,128)(2,1)}, u32[]{:S(2)}, u32[]{:S(2)}) collective-permute-start(bf16[1,2,512,256]{2,3,1,0:T(8,128)(2,1)} %collective-permute-done), channel_id=1, source_target_pairs={{0,4},{4,8},{8,12},{12,16},{16,20},{20,24},{24,28},{1,5},{5,9},{9,... | collective-permute-start | bytes 1572872 | tf_op jit(solution)/shard_map/ppermute | solution.py:13
  76.3 0.0 all-gather.5.cloned.1.call-update
  76.3 0.0 copy-done.7
  76.4 1.0 collective-permute-done.1
  77.3 2.6 %pad_maximum_fusion.1 = bf16[1,2,1536,256]{2,3,1,0:T(8,128)(2,1)} fusion(bf16[1,2,512,256]{2,3,1,0:T(8,128)(2,1)} %copy-done.2, bf16[1,2,512,256]{2,3,1,0:T(8,128)(2,1)} %collective-permute-done, bf16[1,2,512,256]{2,3,1,0:T(8,128)(2,1)} %collective-permute-done.1), kind=kLoop, calls=%fused_computation.25 | loop fusion | flops 4718592 | bytes 3145728 | tf_op jit(solution)/shard_map/concatenate | solution.py:67
  80.0 4.9 %copy.23 = bf16[1,2,1536,256]{3,1,2,0:T(2,128)(2,1)} copy(bf16[1,2,1536,256]{2,3,1,0:T(8,128)(2,1)} %pad_maximum_fusion.1) | data formatting | bytes 3145728
  84.9 5.0 %multiply_reduce_fusion = bf16[2,256,512]{1,0,2:T(2,128)(2,1)} fusion(bf16[2,256,3,512]{1,0,2,3:T(2,128)(2,1)} %bitcast.45, f32[2,256,3]{1,0,2:T(2,128)S(1)} %bitcast_convert_fusion), kind=kLoop, calls=%fused_computation.11 | loop fusion | flops 2097152 | bytes 2103296
  89.9 2.0 %copy.20 = bf16[2,256,512]{2,1,0:T(8,128)(2,1)} copy(bf16[2,256,512]{1,0,2:T(2,128)(2,1)} %multiply_reduce_fusion) | data formatting | bytes 1048576 | tf_op jit(solution)/shard_map/bkltc,tkc->bklc/dot_general | solution.py:26
  91.9 11.8 %collective-permute-start.2 = (bf16[1,2,512,256]{2,3,1,0:T(8,128)(2,1)}, bf16[1,2,512,256]{2,3,1,0:T(8,128)(2,1)S(1)}, u32[]{:S(2)}, u32[]{:S(2)}) collective-permute-start(bf16[1,2,512,256]{2,3,1,0:T(8,128)(2,1)} %bitcast.52), channel_id=1, source_target_pairs={{0,8},{4,12},{8,16},{12,20},{16,24},{20,28},{1,9},{5,13},{9,17},{1... | collective-permute-start | bytes 1572872 | tf_op jit(solution)/shard_map/ppermute | solution.py:13
  103.7 1.6 fusion.10
  105.3 1.0 slice.18
  106.3 0.0 copy-start.6
  106.3 9.7 %collective-permute-done.2 = bf16[1,2,512,256]{2,3,1,0:T(8,128)(2,1)S(1)} collective-permute-done((bf16[1,2,512,256]{2,3,1,0:T(8,128)(2,1)}, bf16[1,2,512,256]{2,3,1,0:T(8,128)(2,1)S(1)}, u32[]{:S(2)}, u32[]{:S(2)}) %collective-permute-start.2) | collective-permute-done | bytes 524320 | tf_op jit(solution)/shard_map/ppermute | solution.py:13
  116.0 1.3 pad_maximum_fusion
  117.3 1.3 fusion.41
  118.6 0.0 copy-done.6
  118.6 3.8 %fusion.42 = f32[2,512]{1,0:T(2,128)S(1)} fusion(pred[512,1536]{1,0:T(8,128)(4,1)} %fusion.10, bf16[512,2,128]{0,2,1:T(8,128)(2,1)S(1)} %bitcast.53, bf16[1536,2,128]{0,2,1:T(8,128)(2,1)} %bitcast.49), kind=kOutput, calls=%fused_computation.63 | convolution fusion | flops 408946176 | bytes 1839104 | tf_op jit(solution)/shard_map/sub | solution.py:52
  122.4 4.6 %fusion.25 = bf16[2,128,512]{2,1,0:T(8,128)(2,1)S(1)} fusion(bf16[1536,2,128]{0,2,1:T(8,128)(2,1)} %bitcast.51, f32[2,512]{1,0:T(2,128)S(1)} %fusion.42, pred[512,1536]{1,0:T(8,128)(4,1)} %fusion.10, bf16[512,2,128]{0,2,1:T(8,128)(2,1)} %bitcast.54, bf16[1536,2,128]{0,2,1:T(8,128)(2,1)} %bitcast.50), kind=kOutput, calls=%fused_computation.32 | convolution fusion | flops 813304320 | bytes 2887680 | tf_op jit(solution)/shard_map/bhqk,bkhd->bqhd/dot_general | solution.py:54
  127.0 0.1 collective-permute-start.3
  127.1 10.0 %collective-permute-done.3 = bf16[1,512,256]{1,2,0:T(8,128)(2,1)S(1)} collective-permute-done((bf16[1,512,256]{1,2,0:T(8,128)(2,1)S(1)}, bf16[1,512,256]{1,2,0:T(8,128)(2,1)S(1)}, u32[]{:S(2)}, u32[]{:S(2)}) %collective-permute-start.3) | collective-permute-done | bytes 262176 | tf_op jit(solution)/shard_map/ppermute | solution.py:78
  137.1 0.0 copy-start.3
  137.1 0.7 copy-done.3
  137.8 0.0 collective-permute-start.4
  137.8 9.3 %collective-permute-done.4 = bf16[1,512,256]{1,2,0:T(8,128)(2,1)} collective-permute-done((bf16[1,512,256]{1,2,0:T(8,128)(2,1)S(1)}, bf16[1,512,256]{1,2,0:T(8,128)(2,1)}, u32[]{:S(2)}, u32[]{:S(2)}) %collective-permute-start.4) | collective-permute-done | bytes 262176 | tf_op jit(solution)/shard_map/ppermute | solution.py:78
  147.1 0.0 collective-permute-start.5
  147.1 0.0 copy-start.4
  147.1 8.7 %collective-permute-done.5 = bf16[1,512,256]{1,2,0:T(8,128)(2,1)} collective-permute-done((bf16[1,512,256]{1,2,0:T(8,128)(2,1)}, bf16[1,512,256]{1,2,0:T(8,128)(2,1)}, u32[]{:S(2)}, u32[]{:S(2)}) %collective-permute-start.5) | collective-permute-done | bytes 262176 | tf_op jit(solution)/shard_map/ppermute | solution.py:78
  155.8 1.7 constant_dynamic-update-slice_fusion.7
  157.4 1.7 constant_dynamic-update-slice_fusion.6
  159.1 1.7 constant_dynamic-update-slice_fusion.5
  160.8 0.7 constant_dynamic-update-slice_fusion.4
  161.5 1.7 constant_dynamic-update-slice_fusion.3
  163.1 1.7 constant_dynamic-update-slice_fusion.2
  164.8 0.0 copy-done.4
  164.8 0.7 constant_dynamic-update-slice_fusion.1
  165.6 0.7 constant_dynamic-update-slice_fusion
  166.3 0.0 all-gather.5.cloned.1.call-done
  166.3 3.1 %fusion.24 = bf16[1,512,512]{2,1,0:T(8,128)(2,1)} fusion(bf16[1024,512]{1,0:T(8,128)(2,1)} %all-gather.5.cloned.1.call-done, bf16[1,512,2048]{1,2,0:T(8,128)(2,1)} %constant_dynamic-update-slice_fusion, s32[]{:T(128)S(6)} %select_n.20), kind=kOutput, calls=%fused_computation.31 | convolution fusion | flops 537133056 | bytes 2621444 | tf_op jit(solution)/shard_map/blr,rc->blc/dot_general | solution.py:84
  (7 shorter events, 0.1 us)
Async XLA Ops:
  7.4 53.7 %copy-start = (bf16[2048,3,256]{2,0,1:T(8,128)(2,1)S(1)}, bf16[2048,3,256]{2,0,1:T(8,128)(2,1)}, u32[]{:S(2)}) copy-start(bf16[2048,3,256]{2,0,1:T(8,128)(2,1)} %param.5) | copy-start | bytes 9437188
  7.4 50.8 %all-gather.3.cloned.1.call-start = ((), (), s32[]{:S(2)}) async-start(), calls=%async_computation | async-start | bytes 2621440 | tf_op jit(solution)/shard_map/all_gather | solution.py:59
  8.1 158.2 %all-gather.5.cloned.1.call-start = ((), (), s32[]{:S(2)}) async-start(), calls=%async_computation.1 | async-start | bytes 1179648 | tf_op jit(solution)/shard_map/all_gather | solution.py:83
  58.1 2.2 %copy-start.1 = (bf16[1,512,2048]{2,1,0:T(8,128)(2,1)S(1)}, bf16[1,512,2048]{2,1,0:T(8,128)(2,1)}, u32[]{:S(2)}) copy-start(bf16[1,512,2048]{2,1,0:T(8,128)(2,1)} %all-gather.3.cloned.1.call-done) | copy-start | bytes 6291460
  61.1 15.3 %copy-start.7 = (bf16[3,2,256]{2,1,0:T(2,128)(2,1)S(1)}, bf16[3,2,256]{2,1,0:T(2,128)(2,1)}, u32[]{:S(2)}) copy-start(bf16[3,2,256]{2,1,0:T(2,128)(2,1)} %param.6) | copy-start | bytes 9220
  63.1 4.1 %copy-start.5 = (bf16[1,3,512,256]{2,3,1,0:T(8,128)(2,1)}, bf16[1,3,512,256]{2,3,1,0:T(8,128)(2,1)S(1)}, u32[]{:S(2)}) copy-start(bf16[1,3,512,256]{2,3,1,0:T(8,128)(2,1)S(1)} %fusion.21) | copy-start | bytes 2359300
  63.1 0.9 copy-start.2
  64.0 3.2 %collective-permute-start = (bf16[1,2,512,256]{2,3,1,0:T(8,128)(2,1)S(1)}, bf16[1,2,512,256]{2,3,1,0:T(8,128)(2,1)}, u32[]{:S(2)}, u32[]{:S(2)}) collective-permute-start(bf16[1,2,512,256]{2,3,1,0:T(8,128)(2,1)S(1)} %slice.16), channel_id=1, source_target_pairs={{0,4},{4,8},{8,12},{12,16},{16,20},{20,24},{24,28},{1,5},{5,9},{9,... | collective-permute-start | bytes 1572872 | tf_op jit(solution)/shard_map/ppermute | solution.py:13
  67.2 10.1 %collective-permute-start.1 = (bf16[1,2,512,256]{2,3,1,0:T(8,128)(2,1)}, bf16[1,2,512,256]{2,3,1,0:T(8,128)(2,1)}, u32[]{:S(2)}, u32[]{:S(2)}) collective-permute-start(bf16[1,2,512,256]{2,3,1,0:T(8,128)(2,1)} %collective-permute-done), channel_id=1, source_target_pairs={{0,4},{4,8},{8,12},{12,16},{16,20},{20,24},{24,28},{1,5},{5,9},{9,... | collective-permute-start | bytes 1572872 | tf_op jit(solution)/shard_map/ppermute | solution.py:13
  91.9 24.1 %collective-permute-start.2 = (bf16[1,2,512,256]{2,3,1,0:T(8,128)(2,1)}, bf16[1,2,512,256]{2,3,1,0:T(8,128)(2,1)S(1)}, u32[]{:S(2)}, u32[]{:S(2)}) collective-permute-start(bf16[1,2,512,256]{2,3,1,0:T(8,128)(2,1)} %bitcast.52), channel_id=1, source_target_pairs={{0,8},{4,12},{8,16},{12,20},{16,24},{20,28},{1,9},{5,13},{9,17},{1... | collective-permute-start | bytes 1572872 | tf_op jit(solution)/shard_map/ppermute | solution.py:13
  106.3 12.3 %copy-start.6 = (bf16[1,1,512,256]{2,3,1,0:T(8,128)(2,1)}, bf16[1,1,512,256]{2,3,1,0:T(8,128)(2,1)S(1)}, u32[]{:S(2)}) copy-start(bf16[1,1,512,256]{2,3,1,0:T(8,128)(2,1)S(1)} %slice.18) | copy-start | bytes 786436
  127.0 10.1 %collective-permute-start.3 = (bf16[1,512,256]{1,2,0:T(8,128)(2,1)S(1)}, bf16[1,512,256]{1,2,0:T(8,128)(2,1)S(1)}, u32[]{:S(2)}, u32[]{:S(2)}) collective-permute-start(bf16[1,512,256]{1,2,0:T(8,128)(2,1)S(1)} %bitcast.46), channel_id=1, source_target_pairs={{0,1},{1,2},{2,3},{3,0},{4,5},{5,6},{6,7},{7,4},{8,9},{9,10},{10,1... | collective-permute-start | bytes 786440 | tf_op jit(solution)/shard_map/ppermute | solution.py:78
  137.1 0.7 copy-start.3
  137.8 9.3 %collective-permute-start.4 = (bf16[1,512,256]{1,2,0:T(8,128)(2,1)S(1)}, bf16[1,512,256]{1,2,0:T(8,128)(2,1)}, u32[]{:S(2)}, u32[]{:S(2)}) collective-permute-start(bf16[1,512,256]{1,2,0:T(8,128)(2,1)S(1)} %collective-permute-done.3), channel_id=1, source_target_pairs={{0,1},{1,2},{2,3},{3,0},{4,5},{5,6},{6,7},{7,4},{8,9},{9,10},{10,1... | collective-permute-start | bytes 786440 | tf_op jit(solution)/shard_map/ppermute | solution.py:78
  147.1 8.7 %collective-permute-start.5 = (bf16[1,512,256]{1,2,0:T(8,128)(2,1)}, bf16[1,512,256]{1,2,0:T(8,128)(2,1)}, u32[]{:S(2)}, u32[]{:S(2)}) collective-permute-start(bf16[1,512,256]{1,2,0:T(8,128)(2,1)} %collective-permute-done.4), channel_id=1, source_target_pairs={{0,1},{1,2},{2,3},{3,0},{4,5},{5,6},{6,7},{7,4},{8,9},{9,10},{10,1... | collective-permute-start | bytes 786440 | tf_op jit(solution)/shard_map/ppermute | solution.py:78
  147.1 17.7 %copy-start.4 = (bf16[1,512,256]{1,2,0:T(8,128)(2,1)S(1)}, bf16[1,512,256]{1,2,0:T(8,128)(2,1)}, u32[]{:S(2)}) copy-start(bf16[1,512,256]{1,2,0:T(8,128)(2,1)} %copy-done.3) | copy-start | bytes 786436
Sparse Core Ops, SparseCore 0:
  9.7 48.3 all-gather.2
Sparse Core Ops, SparseCore 1:
  76.4 23.4 all-gather.4
